TPU v7x, 128 devices: a whole 4x4x4 slice. The times are simulated.
128 devices in a mesh: psg: 32 (over y, z, core), qry: 4 (over x).
Axes of the slice: x: 4, y: 4, z: 4, core: 2. Of those that a mesh axis runs over, the one named last changes fastest.
Arguments:
- queries: bfloat16 [512, 32, 128], P(('psg', 'qry')), may hold values from -6 to 6
- passages: bfloat16 [1024, 256, 128], P('psg'), may hold values from -6 to 6
- candidates: int32 [512, 32], P(('psg', 'qry')), may hold values from 0 to 1023, as said below
- teacher: float32 [512, 32], P(('psg', 'qry')), may hold values from -8 to 8
Outputs:
- pair_loss: float32 [512], P(('psg', 'qry'))
- grad_queries: bfloat16 [512, 32, 128], P(('psg', 'qry'))
- grad_passages: bfloat16 [1024, 256, 128], P('psg', 'qry')
Inputs may be any that keep to these rules, and one draw needn't show every extreme that they name: Passage p lies in block p // 32. Among the 4 x 32 candidates of one device's queries (aligned blocks of 4 rows), at most 10 lie in one passage block; one passage block, the same for all devices, holds exactly 10 of every device's candidates. Candidate ids of one query may repeat.
All inputs are finite; a program needn't handle non-finite values.
Results may differ from a plain program's by a relative error of at most 0.019.
Values may be sent and summed in bfloat16 or wider, within the bound.
A program may use at most 64 MiB of HBM per device.

v0:
```python
import math

import jax
import jax.numpy as jnp
from jax import lax
from jax.experimental import pallas as pl
from jax.experimental.pallas import tpu as pltpu
from jax.sharding import PartitionSpec as P

MESH = pl.DeviceIdType.MESH
BF16, F32, I32 = jnp.bfloat16, jnp.float32, jnp.int32
HIGHEST = lax.Precision.HIGHEST
epsilon = 1e-06
softness_scale = 0.05

OWNERS, GROUPS, CHIPS = 32, 4, 16
QD, QT, C, E, PT, PS = 4, 32, 32, 128, 256, 32
CAP = 10
ROW = QD * QT
SHARE = PT // GROUPS
PER_CHUNK = 4
CHUNKS = (OWNERS * CAP + PS * (PER_CHUNK - 1)) // PER_CHUNK
UNROLL = 8
STEPS = CHUNKS // UNROLL
WIDE = 26
TERM_WIDE = 13
EARLY_TERMS = 4
SIDE = 4
OFFSETS = sorted(
    ((dy, dz) for dy in range(SIDE) for dz in range(SIDE) if dy or dz),
    key=lambda offset: sum(min(d, SIDE - d) for d in offset),
)
LINES = 128
PIECES = 4
PIECE = PS // 2 // PIECES
SLOTS = 512
LANES_PER_SENDER = SLOTS // OWNERS
ORDER = (2, 1, 3, 0)

NT = (((1,), (1,)), ((), ()))
TN = (((0,), (0,)), ((), ()))


def iota(shape, dim):
    return lax.broadcasted_iota(I32, shape, dim)


def dot(a, b, dims=None, precision=None):
    dims = (((1,), (0,)), ((), ())) if dims is None else dims
    return lax.dot_general(a, b, dims, precision=precision, preferred_element_type=F32)


def unit_of(values):
    inverse = lax.rsqrt(jnp.sum(values * values, -1, keepdims=True) + epsilon)
    return values * inverse, inverse


def project(values, gradient):
    unit, inverse = unit_of(values)
    return inverse * (gradient - unit * jnp.sum(unit * gradient, -1, keepdims=True))


def count(mask, axis):
    return jnp.sum(jnp.where(mask, 1, 0), axis, keepdims=True)


def as_row(block):
    return jnp.concatenate([block[index : index + 1] for index in range(block.shape[0])], 1)


def same(a, b):
    return (1 - jnp.minimum((a - b) * (a - b), 1)).astype(F32)


def column_of(row):
    return jnp.broadcast_to(row, (ROW, row.shape[1])).T[:, 0:1]


def slot_tables(ids, teacher):
    lane = iota((1, ROW), 1)
    ids, teacher = as_row(ids), as_row(teacher)
    power = jnp.exp(teacher)
    same_query = (iota((ROW, ROW), 0) // C == iota((ROW, ROW), 1) // C).astype(F32)
    power_sum = dot(jnp.broadcast_to(power, (8, ROW)), same_query, precision=HIGHEST)[0:1]
    target = power / power_sum
    owner = ids >> 5
    code = (lane >> 5) * PS + (ids & (PS - 1)) + 1
    ahead = iota((ROW, ROW), 0) < iota((ROW, ROW), 1)
    rank = count((column_of(owner) == owner) & ahead, 0)
    hits = owner == iota((OWNERS, ROW), 0)
    place = iota((OWNERS, ROW), 1) & (LANES_PER_SENDER - 1)
    codes = jnp.zeros((OWNERS, ROW), I32)
    targets = jnp.zeros((OWNERS, ROW), F32)
    for slot in range(CAP):
        chosen = hits & (rank == slot)
        codes = jnp.where(place == slot, jnp.sum(jnp.where(chosen, code, 0), 1, keepdims=True), codes)
        targets = jnp.where(place == slot, jnp.sum(jnp.where(chosen, target, 0.0), 1, keepdims=True), targets)
    entropy = target * (teacher - jnp.log(power_sum))
    return codes, targets, entropy


def order_slots(codes):
    lane = iota((OWNERS, SLOTS), 1)
    mine = lane >> 4 == iota((OWNERS, SLOTS), 0)
    code = jnp.sum(jnp.where(mine, jnp.concatenate([codes] * 4, 1), 0), 0, keepdims=True) - 1
    live = code >= 0
    local = code >> 5
    query = (iota((1, SLOTS), 1) >> 4) * QD + local
    passage = jnp.where(live, code & (PS - 1), -1)
    ahead = iota((SLOTS, SLOTS), 0) < iota((SLOTS, SLOTS), 1)
    rank = count((column_of(passage) == passage) & ahead, 0)
    index = iota((PS, SLOTS), 0)
    hits = passage == index
    chunks = (count(hits, 1) + (PER_CHUNK - 1)) >> 2
    chunk_row = jnp.sum(jnp.where(lane == index, chunks, 0), 0, keepdims=True)
    first = jnp.sum(jnp.where(lane < index, chunk_row, 0), 1, keepdims=True)
    place = rank + PER_CHUNK * jnp.sum(jnp.where(hits, first, 0), 0, keepdims=True)
    place = jnp.where(live, place, -1)
    ordered = column_of(place) == iota((SLOTS, SLOTS), 1)
    ordered = jnp.sum(jnp.where(ordered, column_of(query) + 1, 0), 0, keepdims=True) - 1
    inside = (first <= lane) & (lane < first + chunks)
    chunk_passage = jnp.sum(jnp.where(inside, index, 0), 0, keepdims=True)
    last = jnp.where(lane == index, jnp.maximum(first + chunks - 1, 0), 0)
    last = jnp.where(lane == index + ROW, jnp.minimum(chunks, 1), last)
    meta = [
        jnp.maximum(ordered, 0),
        chunk_passage,
        jnp.maximum(place, 0),
        jnp.where(live, 1, 0),
        jnp.sum(last, 0, keepdims=True),
    ]
    return meta, place, query


def place_values(place, query, targets):
    mine = iota((OWNERS, SLOTS), 1) >> 4 == iota((OWNERS, SLOTS), 0)
    target = jnp.sum(jnp.where(mine, jnp.concatenate([targets] * 4, 1), 0.0), 0, keepdims=True)
    segment = iota((LINES, ROW), 1) >> 5
    query_at = jnp.full((LINES, ROW), -1, I32)
    target_at = jnp.zeros((LINES, ROW), F32)
    for slot in range(PER_CHUNK):
        chosen = place == iota((LINES, SLOTS), 0) * PER_CHUNK + slot
        found = jnp.sum(jnp.where(chosen, query + 1, 0), 1, keepdims=True) - 1
        query_at = jnp.where(segment == slot, found, query_at)
        found = jnp.sum(jnp.where(chosen, target, 0.0), 1, keepdims=True)
        target_at = jnp.where(segment == slot, found, target_at)
    return query_at, target_at


def kernel(
    q_hbm, ids_hbm, teacher_hbm, passages_hbm,
    loss_out, gq_out, gp_out,
    q_ref, ids_ref, teacher_ref,
    q_all, raw, p_norm, p_turned, code_out, code_in, target_out, target_in, meta_v, meta_s, query_at, target_at, entropy,
    weights, terms, sides, totals_at, grads, own_grads, sums_out, sums_in, part_a, part_b, r2, r1, r3, r0,
    in_left, in_right, from_left, from_right, g_sib_out, g_sib_in, g_out, g_in,
    local_sem, q_send, q_recv, relay_send, relay_recv, code_send, code_recv, target_send, target_recv,
    sums_send, sums_recv, x_send, x_recv, sib_send, sib_recv, g_send, g_recv,
):
    me = lax.axis_index("psg")
    col = lax.axis_index("qry")
    chip, core = me // 2, me % 2
    sibling = chip * 2 + (1 - core)
    right, left = (col + 1) % GROUPS, (col + GROUPS - 1) % GROUPS

    y, z = chip // SIDE, chip % SIDE

    def chip_at(dy, dz):
        return ((y + dy) % SIDE) * SIDE + (z + dz) % SIDE

    far_first = [chip_at(dy, dz) for dy, dz in reversed(OFFSETS)]
    peers = [other * 2 + side for other in far_first for side in (core, 1 - core)] + [sibling]

    small = [
        pltpu.make_async_copy(q_hbm, q_ref, local_sem.at[5]),
        pltpu.make_async_copy(ids_hbm, ids_ref, local_sem.at[6]),
        pltpu.make_async_copy(teacher_hbm, teacher_ref, local_sem.at[7]),
    ]
    for load in small:
        load.start()

    barrier = pltpu.get_barrier_semaphore()
    for other in peers:
        pl.semaphore_signal(barrier, inc=1, device_id={"psg": other}, device_id_type=MESH)
    for side in (left, right):
        pl.semaphore_signal(barrier, inc=1, device_id={"qry": side}, device_id_type=MESH)

    loads = []
    for index, relative in enumerate(ORDER):
        share = (col + relative) % GROUPS
        load = pltpu.make_async_copy(
            passages_hbm.at[:, pl.ds(pl.multiple_of(share * SHARE, SHARE), SHARE), :],
            raw.at[:, pl.ds(index * SHARE, SHARE), :],
            local_sem.at[index],
        )
        load.start()
        loads.append(load)

    small[0].wait()
    q_raw = q_ref[...].astype(F32)
    own_rows = pl.ds(me * QD, QD)
    q_all[own_rows] = unit_of(q_raw)[0].astype(BF16).reshape(QD, QT, E)
    small[1].wait()
    small[2].wait()

    codes, targets, entropy[...] = slot_tables(ids_ref[...], teacher_ref[...])
    for owner in range(OWNERS):
        code_out[owner] = codes[owner : owner + 1]
        target_out[owner] = targets[owner : owner + 1]
    code_in[me] = code_out[me]
    target_in[me] = target_out[me]
    pl.semaphore_wait(barrier, OWNERS - 1 + 2)

    for other in peers:
        pltpu.make_async_remote_copy(
            src_ref=code_out.at[other], dst_ref=code_in.at[me], send_sem=code_send, recv_sem=code_recv,
            device_id={"psg": other}, device_id_type=MESH,
        ).start()

    def send_rows(rows, sender, dy, dz):
        pltpu.make_async_remote_copy(
            src_ref=q_all.at[rows], dst_ref=q_all.at[rows], send_sem=q_send, recv_sem=q_recv.at[sender],
            device_id={"psg": chip_at(dy, dz) * 2 + core}, device_id_type=MESH,
        ).start()

    def relay(rows):
        return pltpu.make_async_remote_copy(
            src_ref=q_all.at[rows], dst_ref=q_all.at[rows], send_sem=relay_send, recv_sem=relay_recv,
            device_id={"psg": sibling}, device_id_type=MESH,
        )

    ahead = 1 + 2 * core
    back = SIDE - ahead
    for dy, dz in (
        (ahead, 0), (0, ahead), (2, 2), (ahead, ahead), (ahead, back), (back, ahead), (back, 0), (0, back), (back, back)
    ):
        send_rows(own_rows, chip, dy, dz)
    relay(own_rows).start()

    for other in peers:
        pltpu.make_async_remote_copy(
            src_ref=target_out.at[other], dst_ref=target_in.at[me], send_sem=target_send, recv_sem=target_recv,
            device_id={"psg": other}, device_id_type=MESH,
        ).start()

    for load in loads:
        load.wait()

    def normalize(begin, end):
        def run(index, carry):
            values = raw[index].astype(F32)
            unit = unit_of(values)[0].astype(BF16)
            p_norm[index] = unit
            p_turned[index] = unit.T
            return carry

        lax.fori_loop(begin, end, run, 0, unroll=4)

    def hand_on(dy, dz, along_y=False, along_z=False):
        sender = chip_at(SIDE - dy, SIDE - dz)
        rows = pl.ds((sender * 2 + core) * QD, QD)
        pltpu.make_async_copy(q_all.at[rows], q_all.at[rows], q_recv.at[sender]).wait()
        if along_y:
            send_rows(rows, sender, ahead, 0)
        if along_z:
            send_rows(rows, sender, 0, ahead)
        relay(rows).start()

    normalize(0, 32)
    hand_on(ahead, 0, along_y=True)
    hand_on(0, ahead, along_z=True)
    hand_on(ahead, ahead, True, True)
    hand_on(ahead, back, along_y=True)
    hand_on(back, ahead, along_z=True)
    hand_on(back, 0)
    hand_on(0, back)
    hand_on(back, back)
    others = pl.ds(0, OWNERS - 1)
    pltpu.make_async_copy(code_in.at[others], code_in.at[others], code_recv).wait()
    meta, place, query_of = order_slots(jnp.concatenate([code_in[owner] for owner in range(OWNERS)], 0))
    for index, row in enumerate(meta):
        meta_v[index : index + 1, :] = row
    meta_v[5:8, :] = jnp.zeros((3, SLOTS), I32)
    hand_on(2, 0)
    hand_on(0, 2)
    to_scalar = pltpu.make_async_copy(meta_v, meta_s, local_sem.at[4])
    to_scalar.start()
    for dy, dz in ((2, ahead), (2, back), (ahead, 2), (back, 2), (2, 2)):
        hand_on(dy, dz)
    pltpu.make_async_copy(target_in.at[others], target_in.at[others], target_recv).wait()
    query_at[...], target_at[...] = place_values(
        place, query_of, jnp.concatenate([target_in[owner] for owner in range(OWNERS)], 0)
    )
    to_scalar.wait()
    half = pl.ds(0, CHIPS * QD)
    pltpu.make_async_copy(q_all.at[half], q_all.at[half], relay_recv).wait()

    factor = math.log2(math.e) / softness_scale

    def gather(chunk):
        return jnp.concatenate([q_all[meta_s[0, chunk * PER_CHUNK + slot]] for slot in range(PER_CHUNK)], 0)

    def forward(step, carry):
        for inner in range(WIDE):
            chunk = step * WIDE + inner
            tokens = p_norm[meta_s[1, chunk]]
            power = jnp.exp2(dot(tokens, gather(chunk), NT) * factor)
            weights[chunk] = power.astype(BF16)
            totals_at[chunk] = jnp.sum(power, 0, keepdims=True)
        return carry

    lax.fori_loop(0, CHUNKS // WIDE, forward, 0)
    lines = [totals_at[chunk] for chunk in range(CHUNKS)] + [jnp.ones((LINES - CHUNKS, ROW), F32)]
    logs = jnp.log(jnp.concatenate(lines, 0))

    lane = iota((LINES, ROW), 1)
    same_slot = (iota((ROW, ROW), 0) >> 5 == iota((ROW, ROW), 1) >> 5).astype(F32)
    score = dot(logs, same_slot, precision=HIGHEST) * softness_scale
    power = jnp.exp(score)
    target = target_at[...]
    shown = target * score
    power_sum = jnp.zeros((1, ROW), F32)
    shown_sum = jnp.zeros((1, ROW), F32)
    for slot in range(PER_CHUNK):
        pick = slice(slot * QT, slot * QT + 1)
        belongs = query_at[:, pick] == lane
        power_sum = power_sum + jnp.sum(jnp.where(belongs, power[:, pick], 0.0), 0, keepdims=True)
        shown_sum = shown_sum + jnp.sum(jnp.where(belongs, shown[:, pick], 0.0), 0, keepdims=True)
    sums_out[0:1, :] = power_sum
    sums_out[1:2, :] = shown_sum
    sums_in[me] = sums_out[...]

    for other in peers:
        pltpu.make_async_remote_copy(
            src_ref=sums_out, dst_ref=sums_in.at[me], send_sem=sums_send, recv_sem=sums_recv,
            device_id={"psg": other}, device_id_type=MESH,
        ).start()

    def scale(chunk, carry):
        inverse = 1.0 / totals_at[chunk]
        weights[chunk] = (weights[chunk].astype(F32) * inverse).astype(BF16)
        return carry

    lax.fori_loop(0, CHUNKS, scale, 0, unroll=13)

    unit = (iota((ROW, ROW), 0) == iota((ROW, ROW), 1)).astype(BF16)

    def query_term(step, carry):
        for inner in range(TERM_WIDE):
            chunk = step * TERM_WIDE + inner
            term = dot(p_turned[meta_s[1, chunk]], weights[chunk]).astype(BF16)
            term = dot(unit, term, NT).astype(BF16)
            terms[pl.ds(chunk * PER_CHUNK, PER_CHUNK)] = term.reshape(PER_CHUNK, QT, E)
        return carry

    lax.fori_loop(0, EARLY_TERMS, query_term, 0)

    pltpu.make_async_copy(sums_in.at[others], sums_in.at[others], sums_recv).wait()
    totals = sums_in[0]
    for owner in range(1, OWNERS):
        totals = totals + sums_in[owner]
    total_row = totals[0:1]
    slot_grads = []
    for slot in range(PER_CHUNK):
        pick = slice(slot * QT, slot * QT + 1)
        query = query_at[:, pick]
        total = jnp.sum(jnp.where(query == lane, total_row, 0.0), 1, keepdims=True)
        likelihood = power[:, pick] / jnp.where(query >= 0, total, 1.0)
        grad = jnp.where(query >= 0, likelihood - target[:, pick], 0.0)
        grads[slot] = jnp.broadcast_to(grad, (LINES, ROW))
        slot_grads.append((query & (QD - 1), grad))

    def passage_step(first, size, parts):
        def run(step, running):
            for inner in range(WIDE):
                chunk = step * WIDE + inner
                keep = same(meta_s[1, chunk], meta_s[1, jnp.maximum(chunk - 1, 0)])
                if first:
                    scale = [
                        jnp.broadcast_to(grads[slot, pl.ds(chunk, 1), :], (QT, E)) for slot in range(PER_CHUNK)
                    ]
                    side = (gather(chunk).astype(F32) * jnp.concatenate(scale, 0)).astype(BF16)
                    sides[chunk] = side
                    values = weights[chunk, 0:size]
                else:
                    side = sides[chunk]
                    values = weights[chunk, PT - size : PT]
                running = running * keep + dot(values, side)
                parts[chunk] = running.astype(BF16)
            return running

        lax.fori_loop(0, CHUNKS // WIDE, run, jnp.zeros((size, E), F32))

    def collect(parts, begin, out):
        def run(index, carry):
            used = meta_s[4, ROW + index].astype(F32)
            part = parts[meta_s[4, index]][begin : begin + SHARE].astype(F32) * used
            out[index] = part.astype(BF16)
            return carry

        lax.fori_loop(0, PS, run, 0, unroll=4)

    def send_piece(kind, piece, side, source, begin, target_ref, target_begin):
        index = kind * PIECES + piece
        copy = pltpu.make_async_remote_copy(
            src_ref=source.at[pl.ds(begin + piece * PIECE, PIECE)],
            dst_ref=target_ref.at[pl.ds(target_begin + piece * PIECE, PIECE)],
            send_sem=x_send.at[index],
            recv_sem=x_recv.at[index],
            device_id={"qry": side},
            device_id_type=MESH,
        )
        copy.start()
        return copy

    def send_pieces(kind, *rest):
        return [send_piece(kind, piece, *rest) for piece in range(PIECES)]

    passage_step(True, SHARE, part_a)
    collect(part_a, 0, r2)
    onward_right = send_pieces(0, right, r2, 0, in_left, 0)
    onward_left = send_pieces(1, left, r2, PS // 2, in_right, 0)
    passage_step(False, 3 * SHARE, part_b)
    collect(part_b, 0, r1)
    direct_right = send_pieces(2, right, r1, PS // 2, from_left, PS // 2)
    collect(part_b, SHARE, r3)
    direct_left = send_pieces(3, left, r3, 0, from_right, 0)
    collect(part_b, 2 * SHARE, r0)

    def query_block(sender):
        sums = [jnp.zeros((QT, E), F32) for _ in range(QD)]
        for slot in range(CAP):
            place = meta_s[2, sender * LANES_PER_SENDER + slot]
            live = meta_s[3, sender * LANES_PER_SENDER + slot].astype(F32)
            term = terms[place].astype(F32) * live
            for query in range(QD):
                sums[query] = sums[query] + term * own_grads[query, place & 3, pl.ds(place >> 2, 1), :]
        return jnp.concatenate(sums, 0)

    def for_sibling(index, carry):
        g_sib_out[index] = query_block(index * 2 + (1 - core)).astype(BF16)
        return carry

    def for_chips(index, carry):
        g_out[index] = query_block(index * 2 + core).astype(BF16)
        return carry

    loss_row = jnp.log(total_row) - totals[1:2]
    one_lane = iota((1, ROW), 1)
    loss = jnp.zeros((1, ROW), F32)
    for query in range(QD):
        mine = jnp.sum(jnp.where(one_lane == me * QD + query, loss_row, 0.0), 1, keepdims=True)
        mine = mine + jnp.sum(jnp.where(one_lane >> 5 == query, entropy[...], 0.0), 1, keepdims=True)
        loss = jnp.where(one_lane == query, mine, loss)
    loss_out[...] = loss
    lax.fori_loop(EARLY_TERMS, CHUNKS // TERM_WIDE, query_term, 0)
    for slot, (local, grad) in enumerate(slot_grads):
        for query in range(QD):
            mine = jnp.where(local == query, grad, 0.0)
            own_grads[query, slot] = jnp.broadcast_to(mine, (LINES, ROW))

    lax.fori_loop(0, CHIPS, for_sibling, 0)
    to_sibling = pltpu.make_async_remote_copy(
        src_ref=g_sib_out, dst_ref=g_sib_in, send_sem=sib_send, recv_sem=sib_recv,
        device_id={"psg": sibling}, device_id_type=MESH,
    )
    to_sibling.start()
    lax.fori_loop(0, CHIPS, for_chips, 0)
    to_sibling.wait_recv()

    def add_sibling(index, carry):
        g_out[index] = (g_out[index].astype(F32) + g_sib_in[index].astype(F32)).astype(BF16)
        return carry

    lax.fori_loop(0, CHIPS, add_sibling, 0)

    for other in far_first:
        pltpu.make_async_remote_copy(
            src_ref=g_out.at[other], dst_ref=g_in.at[chip], send_sem=g_send, recv_sem=g_recv,
            device_id={"psg": other * 2 + core}, device_id_type=MESH,
        ).start()
    g_in[chip] = g_out[chip]

    def merge(incoming, out, begin, piece):
        for index in range(piece * PIECE, (piece + 1) * PIECE):
            both = out[begin + index].astype(F32) + incoming[index].astype(F32)
            out[begin + index] = both.astype(BF16)

    final_right, final_left = [], []
    for piece in range(PIECES):
        onward_right[piece].wait_recv()
        merge(in_left, r1, 0, piece)
        onward_left[piece].wait_recv()
        merge(in_right, r3, PS // 2, piece)
        final_right.append(send_piece(4, piece, right, r1, 0, from_left, 0))
        final_left.append(send_piece(5, piece, left, r3, PS // 2, from_right, PS // 2))

    fewer = pl.ds(0, CHIPS - 1)
    pltpu.make_async_copy(g_in.at[fewer], g_in.at[fewer], g_recv).wait()
    gradient = jnp.zeros((ROW, E), F32)
    for index in range(CHIPS):
        gradient = gradient + g_in[index].astype(F32)
    gq_out[...] = project(q_ref[...].astype(F32), gradient).astype(BF16)

    def finish(index):
        gradient = r0[index].astype(F32) + from_left[index].astype(F32) + from_right[index].astype(F32)
        values = raw[index, 3 * SHARE : 4 * SHARE, :].astype(F32)
        gp_out[index] = project(values, gradient).astype(BF16)

    for copy in (*direct_right, *direct_left):
        copy.wait_recv()
    for piece in range(PIECES):
        final_right[piece].wait_recv()
        final_left[piece].wait_recv()
        for base in (piece * PIECE, PS // 2 + piece * PIECE):
            for inner in range(PIECE):
                finish(base + inner)

    for copy in (*onward_right, *onward_left, *direct_right, *direct_left, *final_right, *final_left, to_sibling):
        copy.wait_send()
    pltpu.make_async_copy(code_in.at[others], code_in.at[others], code_send).wait()
    pltpu.make_async_copy(target_in.at[others], target_in.at[others], target_send).wait()
    pltpu.make_async_copy(sums_in.at[others], sums_in.at[others], sums_send).wait()
    pltpu.make_async_copy(g_in.at[fewer], g_in.at[fewer], g_send).wait()
    sent = pl.ds(0, (CHIPS - 1) * QD)
    pltpu.make_async_copy(q_all.at[sent], q_all.at[sent], q_send).wait()
    pltpu.make_async_copy(q_all.at[half], q_all.at[half], relay_send).wait()


def deliver(loss_in, gq_in, gp_in, loss_out, gq_out, gp_out):
    loss_out[...] = loss_in[:, 0:QD]
    gq_out[...] = gq_in[...]
    gp_out[...] = gp_in[...]


def step(queries, ids, teacher, passages):
    dma = pltpu.SemaphoreType.DMA
    vmem = pltpu.VMEM
    share = (PS, SHARE, E)
    half_share = (PS // 2, SHARE, E)
    owner_block = (CHIPS, ROW, E)
    return pl.pallas_call(
        kernel,
        out_shape=(
            jax.ShapeDtypeStruct((1, ROW), F32),
            jax.ShapeDtypeStruct((ROW, E), BF16),
            jax.ShapeDtypeStruct(share, BF16),
        ),
        in_specs=[pl.BlockSpec(memory_space=pltpu.HBM)] * 4,
        out_specs=(pl.BlockSpec(memory_space=pltpu.VMEM),) * 3,
        scratch_shapes=[
            vmem((ROW, E), BF16),
            vmem((QD, C), I32),
            vmem((QD, C), F32),
            vmem((OWNERS * QD, QT, E), BF16),
            vmem((PS, PT, E), BF16),
            vmem((PS, PT, E), BF16),
            vmem((PS, E, PT), BF16),
            vmem((OWNERS, 1, ROW), I32),
            vmem((OWNERS, 1, ROW), I32),
            vmem((OWNERS, 1, ROW), F32),
            vmem((OWNERS, 1, ROW), F32),
            vmem((8, SLOTS), I32),
            pltpu.SMEM((8, SLOTS), I32),
            vmem((LINES, ROW), I32),
            vmem((LINES, ROW), F32),
            vmem((1, ROW), F32),
            vmem((CHUNKS, PT, ROW), BF16),
            vmem((CHUNKS * PER_CHUNK, QT, E), BF16),
            vmem((CHUNKS, ROW, E), BF16),
            vmem((CHUNKS, 1, ROW), F32),
            vmem((PER_CHUNK, LINES, ROW), F32),
            vmem((QD, PER_CHUNK, LINES, ROW), F32),
            vmem((2, ROW), F32),
            vmem((OWNERS, 2, ROW), F32),
            vmem((CHUNKS, SHARE, E), BF16),
            vmem((CHUNKS, 3 * SHARE, E), BF16),
            vmem(share, BF16),
            vmem(share, BF16),
            vmem(share, BF16),
            vmem(share, BF16),
            vmem(half_share, BF16),
            vmem(half_share, BF16),
            vmem(share, BF16),
            vmem(share, BF16),
            vmem(owner_block, BF16),
            vmem(owner_block, BF16),
            vmem(owner_block, BF16),
            vmem(owner_block, BF16),
            dma((8,)),
            dma,
            dma((CHIPS,)),
            dma,
            dma,
            dma,
            dma,
            dma,
            dma,
            dma,
            dma,
            dma((6 * PIECES,)),
            dma((6 * PIECES,)),
            dma,
            dma,
            dma,
            dma,
        ],
        compiler_params=pltpu.CompilerParams(collective_id=0, has_side_effects=True, vmem_limit_bytes=44 << 20),
    )(*(pltpu.with_memory_space_constraint(value, pltpu.HBM) for value in (queries, ids, teacher, passages)))


def shards(queries, passages, candidates, teacher):
    loss, grad_queries, grad_passages = step(queries.reshape(ROW, E), candidates, teacher, passages)
    loss, grad_queries, grad_passages = pl.pallas_call(
        deliver,
        out_shape=(
            jax.ShapeDtypeStruct((1, QD), F32),
            jax.ShapeDtypeStruct(grad_queries.shape, BF16),
            jax.ShapeDtypeStruct(grad_passages.shape, BF16),
        ),
        in_specs=[pl.BlockSpec(memory_space=pltpu.VMEM)] * 3,
        out_specs=(pl.BlockSpec(memory_space=pltpu.VMEM),) * 3,
        compiler_params=pltpu.CompilerParams(vmem_limit_bytes=4 << 20),
    )(loss, grad_queries, grad_passages)
    return loss.reshape(QD), grad_queries.reshape(QD, QT, E), grad_passages


def solution(mesh):
    placed = (
        P(("psg", "qry"), None, None),
        P("psg", None, None),
        P(("psg", "qry"), None),
        P(("psg", "qry"), None),
    )
    return jax.shard_map(
        shards,
        mesh=mesh,
        in_specs=placed,
        out_specs=(P(("psg", "qry")), P(("psg", "qry"), None, None), P("psg", "qry", None)),
        check_vma=False,
    )
```

profile of v0, /device:TPU:1, one launch (start us, length us, event | category | flops | bytes accessed | tf_op | source)
XLA Modules:
  0.0 52.0 jit_solution(556898452516372474)
XLA Ops:
  0.6 50.5 %shard_map.67 = (f32[1,128]{1,0:T(1,128)S(1)}, bf16[128,128]{1,0:T(8,128)(2,1)S(1)}, bf16[32,64,128]{2,1,0:T(8,128)(2,1)S(1)}) custom-call(bf16[128,128]{1,0:T(8,128)(2,1)} %bitcast.3, s32[4,32]{1,0:T(4,128)} %ids_hbm.1, f32[4,32]{1,0:T(4,128)} %teacher_hbm.1, bf16[32,256,128]{2,1,0:T(8,128)(2,1)} %passages_hbm.1), custom_call_target="tpu_custom_call" | custom-call | tf_op jit(solution)/shard_map/pallas_call | solution.py:542
  51.1 0.8 %shard_map.68 = (f32[1,4]{1,0:T(1,128)}, bf16[128,128]{1,0:T(8,128)(2,1)}, bf16[32,64,128]{2,1,0:T(8,128)(2,1)}) custom-call(f32[1,128]{1,0:T(1,128)S(1)} %get-tuple-element.9.loss_in, bf16[128,128]{1,0:T(8,128)(2,1)S(1)} %get-tuple-element.10.gq_in, bf16[32,64,128]{2,1,0:T(8,128)(2,1)S(1)} %get-tuple-element.11.gp_in), custom_call_target="tpu_custom_call" | custom-call | tf_op jit(solution)/shard_map/pallas_call | solution.py:614
where the time goes:
time: 52.1 us; the launch traced here: 52 us
  Pallas kernels  51.3 us (98%)
  between operations  0.64 us (1%)
    pallas_call x1, Pallas kernels, step(): pl.pallas_call(kernel, out_shape=(jax.ShapeDtypeStruct((1, ROW), F32), ja...  50.5 us

commit v1 on v0

--- a/solution.py
+++ b/solution.py
@@ -24,7 +24,7 @@
 STEPS = CHUNKS // UNROLL
 WIDE = 26
 TERM_WIDE = 13
-EARLY_TERMS = 4
+EARLY_TERMS = 3
 SIDE = 4
 OFFSETS = sorted(
     ((dy, dz) for dy in range(SIDE) for dz in range(SIDE) if dy or dz),
@@ -343,14 +343,11 @@
 
     lax.fori_loop(0, CHUNKS, scale, 0, unroll=13)
 
-    unit = (iota((ROW, ROW), 0) == iota((ROW, ROW), 1)).astype(BF16)
-
     def query_term(step, carry):
         for inner in range(TERM_WIDE):
             chunk = step * TERM_WIDE + inner
             term = dot(p_turned[meta_s[1, chunk]], weights[chunk]).astype(BF16)
-            term = dot(unit, term, NT).astype(BF16)
-            terms[pl.ds(chunk * PER_CHUNK, PER_CHUNK)] = term.reshape(PER_CHUNK, QT, E)
+            terms[pl.ds(chunk * PER_CHUNK, PER_CHUNK)] = term.T.reshape(PER_CHUNK, QT, E)
         return carry
 
     lax.fori_loop(0, EARLY_TERMS, query_term, 0)

time: 52.1 us -> 50.3 us (0.965)
  Pallas kernels: 51.3 us -> 49.5 us
    pallas_call x1, Pallas kernels: 50.5 us -> 48.7 us  [step(): pl.pallas_call(kernel, out_shape=(jax.ShapeDtypeStruct((1, ROW), F32), ja...]
where the time goes in v1:
time: 50.3 us; the launch traced here: 50.2 us
  Pallas kernels  49.5 us (98%)
  between operations  0.64 us (1%)
    pallas_call x1, Pallas kernels, step(): pl.pallas_call(kernel, out_shape=(jax.ShapeDtypeStruct((1, ROW), F32), ja...  48.7 us

profile of v1, /device:TPU:1, one launch (start us, length us, event | category | flops | bytes accessed | tf_op | source)
XLA Modules:
  0.0 50.2 jit_solution(10128622264671624521)
XLA Ops:
  0.6 48.7 %shard_map.67 = (f32[1,128]{1,0:T(1,128)S(1)}, bf16[128,128]{1,0:T(8,128)(2,1)S(1)}, bf16[32,64,128]{2,1,0:T(8,128)(2,1)S(1)}) custom-call(bf16[128,128]{1,0:T(8,128)(2,1)} %bitcast.3, s32[4,32]{1,0:T(4,128)} %ids_hbm.1, f32[4,32]{1,0:T(4,128)} %teacher_hbm.1, bf16[32,256,128]{2,1,0:T(8,128)(2,1)} %passages_hbm.1), custom_call_target="tpu_custom_call" | custom-call | tf_op jit(solution)/shard_map/pallas_call | solution.py:539
  49.3 0.8 %shard_map.68 = (f32[1,4]{1,0:T(1,128)}, bf16[128,128]{1,0:T(8,128)(2,1)}, bf16[32,64,128]{2,1,0:T(8,128)(2,1)}) custom-call(f32[1,128]{1,0:T(1,128)S(1)} %get-tuple-element.9.loss_in, bf16[128,128]{1,0:T(8,128)(2,1)S(1)} %get-tuple-element.10.gq_in, bf16[32,64,128]{2,1,0:T(8,128)(2,1)S(1)} %get-tuple-element.11.gp_in), custom_call_target="tpu_custom_call" | custom-call | tf_op jit(solution)/shard_map/pallas_call | solution.py:611

commit v2 on v1

--- a/solution.py
+++ b/solution.py
@@ -22,7 +22,7 @@
 CHUNKS = (OWNERS * CAP + PS * (PER_CHUNK - 1)) // PER_CHUNK
 UNROLL = 8
 STEPS = CHUNKS // UNROLL
-WIDE = 26
+WIDE = 52
 TERM_WIDE = 13
 EARLY_TERMS = 3
 SIDE = 4
@@ -388,11 +388,14 @@
 
         lax.fori_loop(0, CHUNKS // WIDE, run, jnp.zeros((size, E), F32))
 
+    def collect_one(parts, begin, out, index):
+        used = meta_s[4, ROW + index].astype(F32)
+        part = parts[meta_s[4, index]][begin : begin + SHARE].astype(F32) * used
+        out[index] = part.astype(BF16)
+
     def collect(parts, begin, out):
         def run(index, carry):
-            used = meta_s[4, ROW + index].astype(F32)
-            part = parts[meta_s[4, index]][begin : begin + SHARE].astype(F32) * used
-            out[index] = part.astype(BF16)
+            collect_one(parts, begin, out, index)
             return carry
 
         lax.fori_loop(0, PS, run, 0, unroll=4)
@@ -402,7 +405,7 @@
         copy = pltpu.make_async_remote_copy(
             src_ref=source.at[pl.ds(begin + piece * PIECE, PIECE)],
             dst_ref=target_ref.at[pl.ds(target_begin + piece * PIECE, PIECE)],
-            send_sem=x_send.at[index],
+            send_sem=x_send,
             recv_sem=x_recv.at[index],
             device_id={"qry": side},
             device_id_type=MESH,
@@ -414,9 +417,13 @@
         return [send_piece(kind, piece, *rest) for piece in range(PIECES)]
 
     passage_step(True, SHARE, part_a)
-    collect(part_a, 0, r2)
-    onward_right = send_pieces(0, right, r2, 0, in_left, 0)
-    onward_left = send_pieces(1, left, r2, PS // 2, in_right, 0)
+    onward_right, onward_left = [], []
+    for piece in range(PIECES):
+        for index in range(piece * PIECE, (piece + 1) * PIECE):
+            collect_one(part_a, 0, r2, index)
+            collect_one(part_a, 0, r2, PS // 2 + index)
+        onward_right.append(send_piece(0, piece, right, r2, 0, in_left, 0))
+        onward_left.append(send_piece(1, piece, left, r2, PS // 2, in_right, 0))
     passage_step(False, 3 * SHARE, part_b)
     collect(part_b, 0, r1)
     direct_right = send_pieces(2, right, r1, PS // 2, from_left, PS // 2)
@@ -456,14 +463,15 @@
             mine = jnp.where(local == query, grad, 0.0)
             own_grads[query, slot] = jnp.broadcast_to(mine, (LINES, ROW))
 
-    lax.fori_loop(0, CHIPS, for_sibling, 0)
-    to_sibling = pltpu.make_async_remote_copy(
-        src_ref=g_sib_out, dst_ref=g_sib_in, send_sem=sib_send, recv_sem=sib_recv,
-        device_id={"psg": sibling}, device_id_type=MESH,
-    )
-    to_sibling.start()
+    for begin in range(0, CHIPS, SIDE):
+        lax.fori_loop(begin, begin + SIDE, for_sibling, 0)
+        blocks = pl.ds(begin, SIDE)
+        pltpu.make_async_remote_copy(
+            src_ref=g_sib_out.at[blocks], dst_ref=g_sib_in.at[blocks], send_sem=sib_send, recv_sem=sib_recv,
+            device_id={"psg": sibling}, device_id_type=MESH,
+        ).start()
     lax.fori_loop(0, CHIPS, for_chips, 0)
-    to_sibling.wait_recv()
+    pltpu.make_async_copy(g_sib_in, g_sib_in, sib_recv).wait()
 
     def add_sibling(index, carry):
         g_out[index] = (g_out[index].astype(F32) + g_sib_in[index].astype(F32)).astype(BF16)
@@ -513,8 +521,9 @@
             for inner in range(PIECE):
                 finish(base + inner)
 
-    for copy in (*onward_right, *onward_left, *direct_right, *direct_left, *final_right, *final_left, to_sibling):
-        copy.wait_send()
+    sent_pieces = pl.ds(0, 6 * PIECES)
+    pltpu.make_async_copy(weights.at[sent_pieces], weights.at[sent_pieces], x_send).wait()
+    pltpu.make_async_copy(g_sib_out, g_sib_out, sib_send).wait()
     pltpu.make_async_copy(code_in.at[others], code_in.at[others], code_send).wait()
     pltpu.make_async_copy(target_in.at[others], target_in.at[others], target_send).wait()
     pltpu.make_async_copy(sums_in.at[others], sums_in.at[others], sums_send).wait()
@@ -595,7 +604,7 @@
             dma,
             dma,
             dma,
-            dma((6 * PIECES,)),
+            dma,
             dma((6 * PIECES,)),
             dma,
             dma,

time: 50.3 us -> 49.5 us (0.984)
  Pallas kernels: 49.5 us -> 48.7 us
    pallas_call x1, Pallas kernels: 48.7 us -> 47.8 us  [step(): pl.pallas_call(kernel, out_shape=(jax.ShapeDtypeStruct((1, ROW), F32), ja...]
where the time goes in v2:
time: 49.5 us; the launch traced here: 49.3 us
  Pallas kernels  48.7 us (98%)
  between operations  0.64 us (1%)
    pallas_call x1, Pallas kernels, step(): pl.pallas_call(kernel, out_shape=(jax.ShapeDtypeStruct((1, ROW), F32), ja...  47.8 us

profile of v2, /device:TPU:1, one launch (start us, length us, event | category | flops | bytes accessed | tf_op | source)
XLA Modules:
  0.0 49.3 jit_solution(1619887251309136545)
XLA Ops:
  0.6 47.8 %shard_map.67 = (f32[1,128]{1,0:T(1,128)S(1)}, bf16[128,128]{1,0:T(8,128)(2,1)S(1)}, bf16[32,64,128]{2,1,0:T(8,128)(2,1)S(1)}) custom-call(bf16[128,128]{1,0:T(8,128)(2,1)} %bitcast.3, s32[4,32]{1,0:T(4,128)} %ids_hbm.1, f32[4,32]{1,0:T(4,128)} %teacher_hbm.1, bf16[32,256,128]{2,1,0:T(8,128)(2,1)} %passages_hbm.1), custom_call_target="tpu_custom_call" | custom-call | tf_op jit(solution)/shard_map/pallas_call | solution.py:548
  48.5 0.8 %shard_map.68 = (f32[1,4]{1,0:T(1,128)}, bf16[128,128]{1,0:T(8,128)(2,1)}, bf16[32,64,128]{2,1,0:T(8,128)(2,1)}) custom-call(f32[1,128]{1,0:T(1,128)S(1)} %get-tuple-element.9.loss_in, bf16[128,128]{1,0:T(8,128)(2,1)S(1)} %get-tuple-element.10.gq_in, bf16[32,64,128]{2,1,0:T(8,128)(2,1)S(1)} %get-tuple-element.11.gp_in), custom_call_target="tpu_custom_call" | custom-call | tf_op jit(solution)/shard_map/pallas_call | solution.py:620

commit v3 on v2

--- a/solution.py
+++ b/solution.py
@@ -22,7 +22,7 @@
 CHUNKS = (OWNERS * CAP + PS * (PER_CHUNK - 1)) // PER_CHUNK
 UNROLL = 8
 STEPS = CHUNKS // UNROLL
-WIDE = 52
+WIDE = 104
 TERM_WIDE = 13
 EARLY_TERMS = 3
 SIDE = 4
@@ -353,9 +353,10 @@
     lax.fori_loop(0, EARLY_TERMS, query_term, 0)
 
     pltpu.make_async_copy(sums_in.at[others], sums_in.at[others], sums_recv).wait()
-    totals = sums_in[0]
-    for owner in range(1, OWNERS):
-        totals = totals + sums_in[owner]
+    totals = [sums_in[owner] for owner in range(OWNERS)]
+    while len(totals) > 1:
+        totals = [first + second for first, second in zip(totals[::2], totals[1::2])]
+    totals = totals[0]
     total_row = totals[0:1]
     slot_grads = []
     for slot in range(PER_CHUNK):

time: 49.5 us -> 49.1 us (level)
  no operation moved by 1% of the time
where the time goes in v3:
time: 49.1 us; the launch traced here: 48.9 us
  Pallas kernels  48.3 us (98%)
  between operations  0.64 us (1%)
    pallas_call x1, Pallas kernels, step(): pl.pallas_call(kernel, out_shape=(jax.ShapeDtypeStruct((1, ROW), F32), ja...  47.5 us

profile of v3, /device:TPU:1, one launch (start us, length us, event | category | flops | bytes accessed | tf_op | source)
XLA Modules:
  0.0 48.9 jit_solution(1789406272613479200)
XLA Ops:
  0.6 47.5 %shard_map.67 = (f32[1,128]{1,0:T(1,128)S(1)}, bf16[128,128]{1,0:T(8,128)(2,1)S(1)}, bf16[32,64,128]{2,1,0:T(8,128)(2,1)S(1)}) custom-call(bf16[128,128]{1,0:T(8,128)(2,1)} %bitcast.3, s32[4,32]{1,0:T(4,128)} %ids_hbm.1, f32[4,32]{1,0:T(4,128)} %teacher_hbm.1, bf16[32,256,128]{2,1,0:T(8,128)(2,1)} %passages_hbm.1), custom_call_target="tpu_custom_call" | custom-call | tf_op jit(solution)/shard_map/pallas_call | solution.py:549
  48.1 0.8 %shard_map.68 = (f32[1,4]{1,0:T(1,128)}, bf16[128,128]{1,0:T(8,128)(2,1)}, bf16[32,64,128]{2,1,0:T(8,128)(2,1)}) custom-call(f32[1,128]{1,0:T(1,128)S(1)} %get-tuple-element.9.loss_in, bf16[128,128]{1,0:T(8,128)(2,1)S(1)} %get-tuple-element.10.gq_in, bf16[32,64,128]{2,1,0:T(8,128)(2,1)S(1)} %get-tuple-element.11.gp_in), custom_call_target="tpu_custom_call" | custom-call | tf_op jit(solution)/shard_map/pallas_call | solution.py:621
